TPU v7x, 256 devices: a whole 4x4x8 slice. The times are simulated.
256 devices in a mesh: slab: 64 (over y, x_lo, z), grp: 4 (over x_hi, core).
Axes of the slice: x: 4 (x_hi: 2, x_lo: 2; x = x_hi * 2 + x_lo), y: 4, z: 8, core: 2. Of those that a mesh axis runs over, the one named last changes fastest.
Arguments:
- tiles: bfloat16 [768, 27, 36864], P(('slab', 'grp')), may hold values from -0.0390625 to 0.0390625
- neighbours: int32 [768, 27], P('slab'), may hold values from 0 to 767, as said below
- t_cur: bfloat16 [768, 192, 512], P('slab', None, 'grp'), may hold values from -6 to 6
- t_prev: float32 [768, 192, 512], P('slab', None, 'grp'), may hold values from -6 to 6
- probes: float32 [768, 192, 512], P('slab', None, 'grp'), may hold values from -18 to 18
Outputs:
- t_next: float32 [768, 192, 512], P('slab', None, 'grp')
- moments: float32 [2, 512], P(None, 'grp')
Inputs may be any that keep to these rules, and one draw needn't show every extreme that they name: Block b lies in slab b // 12; each of its neighbours lies in the same slab or in one of the two slabs beside it, the last slab being beside the first.
All inputs are finite; a program needn't handle non-finite values.
Results may differ from a plain program's by a relative error of at most 0.0003.
Values may be sent and summed in bfloat16 or wider, within the bound.
A program may use at most 192 MiB of HBM per device.

v0:
```python
import math

import jax
import jax.numpy as jnp
from jax import lax
from jax.sharding import PartitionSpec as P


def with_halo(value, sides, width):
    for axis, dim in sides:
        size, length = (lax.axis_size(axis), value.shape[dim])
        up = [(i, (i + 1) % size) for i in range(size)]
        down = [(j, i) for i, j in up]
        last = lax.slice_in_dim(value, length - width, length, axis=dim)
        leading = lax.slice_in_dim(value, 0, width, axis=dim)
        before = lax.ppermute(last, axis, up)
        after = lax.ppermute(leading, axis, down)
        value = jnp.concatenate([before, value, after], axis=dim)
    return value


def apply_rows(tile_rows, padded, locals_rows):
    width = padded.shape[1]
    squares = tile_rows.reshape(tile_rows.shape[:2] + (width, width))
    near = jnp.take(padded, locals_rows.reshape(-1), axis=0)
    near = near.reshape(locals_rows.shape + padded.shape[1:])
    return jnp.einsum("bkrc,bkcp->brp", squares, near, preferred_element_type=jnp.float32)


def shards(tiles, neighbours, t_cur, t_prev, probes):
    blocks_slab = t_cur.shape[0]
    slab_count = lax.axis_size("slab")
    my_slab = lax.axis_index("slab")
    slab_near = neighbours // blocks_slab
    local_ids = (slab_near - my_slab + 1) % slab_count * blocks_slab + neighbours % blocks_slab
    rows_dev = tiles.shape[0]
    mine = lax.dynamic_slice_in_dim(local_ids, lax.axis_index("grp") * rows_dev, rows_dev, 0)
    whole = lax.all_gather(t_cur, "grp", axis=2, tiled=True)
    padded = with_halo(whole, (("slab", 0),), blocks_slab)
    rows_image = apply_rows(tiles, padded, mine)
    image = lax.all_to_all(rows_image, "grp", split_axis=2, concat_axis=0, tiled=True)
    t_next = 2.0 * image - t_prev
    first = jnp.sum(probes * t_next, axis=(0, 1))
    second = jnp.sum(t_cur.astype(jnp.float32) * t_next, axis=(0, 1))
    first, second = lax.psum((first, second), "slab")
    factor = 1.0 / math.sqrt(slab_count * blocks_slab * t_cur.shape[1])
    moments = jnp.stack([first, second]) * factor
    return (t_next, moments)


def solution(mesh):
    placed = (
        P(("slab", "grp"), None, None),
        P("slab", None),
        P("slab", None, "grp"),
        P("slab", None, "grp"),
        P("slab", None, "grp"),
    )
    return jax.shard_map(
        shards,
        mesh=mesh,
        in_specs=placed,
        out_specs=(P("slab", None, "grp"), P(None, "grp")),
        check_vma=False,
    )
```

profile of v0, /device:TPU:0, one launch (start us, length us, event | category | flops | bytes accessed | tf_op | source)
XLA Modules:
  0.0 328.1 jit_solution(8495705729886352172)
XLA Ops:
  7.2 0.0 all-gather.2.cloned.1.call-start
  7.2 0.7 all-gather.2.cloned.1.call-update
  7.9 34.1 %all-gather.2.cloned.1.call-done = bf16[12,192,512]{2,1,0:T(8,128)(2,1)} async-done(((bf16[12,192,128]{2,1,0:T(8,128)(2,1)}), bf16[12,192,512]{2,1,0:T(8,128)(2,1)}) %all-gather.2.cloned.1.call-update) | async-done | bytes 2359312 | tf_op jit(solution)/shard_map/all_gather | solution.py:38
  42.0 1.6 collective-permute-start
  43.6 4.7 %collective-permute-start.1 = (bf16[12,192,512]{2,1,0:T(8,128)(2,1)}, bf16[12,192,512]{2,1,0:T(8,128)(2,1)}, u32[]{:S(2)}, u32[]{:S(2)}) collective-permute-start(bf16[12,192,512]{2,1,0:T(8,128)(2,1)} %all-gather.2.cloned.1.call-done), channel_id=1, source_target_pairs={{4,0},{8,4},{12,8},{16,12},{20,16},{24,20},{28,24},{32,28},{36,32}... | collective-permute-start | bytes 7077896 | tf_op jit(solution)/shard_map/ppermute | solution.py:17
  48.3 0.7 broadcast_compare_fusion
  49.0 0.7 fusion.16
  49.7 0.1 reshape.51
  49.8 0.0 copy-start
  49.8 12.2 %reshape.52 = bf16[3,27,192,192]{3,2,1,0:T(8,128)(2,1)} reshape(bf16[3,27,36864]{2,1,0:T(8,128)(2,1)} %param.5) | data formatting | bytes 11943936 | tf_op jit(solution)/shard_map/reshape | solution.py:24
  62.0 37.9 %collective-permute-done = bf16[12,192,512]{2,1,0:T(8,128)(2,1)} collective-permute-done((bf16[12,192,512]{2,1,0:T(8,128)(2,1)}, bf16[12,192,512]{2,1,0:T(8,128)(2,1)}, u32[]{:S(2)}, u32[]{:S(2)}) %collective-permute-start) | collective-permute-done | bytes 2359328 | tf_op jit(solution)/shard_map/ppermute | solution.py:16
  100.0 0.0 collective-permute-done.1
  100.0 0.0 copy-done
  100.0 5.9 %pad_maximum_fusion = bf16[36,192,512]{2,1,0:T(8,128)(2,1)} fusion(bf16[12,192,512]{2,1,0:T(8,128)(2,1)} %collective-permute-done.1, bf16[12,192,512]{2,1,0:T(8,128)(2,1)S(1)} %copy-done, bf16[12,192,512]{2,1,0:T(8,128)(2,1)} %collective-permute-done), kind=kLoop, calls=%fused_computation.5 | loop fusion | flops 7077888 | bytes 14155776 | tf_op jit(solution)/shard_map/concatenate | solution.py:18
  105.8 11.3 %gather_fusion = bf16[81,192,512]{2,1,0:T(8,128)(2,1)} fusion(bf16[36,192,512]{2,1,0:T(8,128)(2,1)} %pad_maximum_fusion, s32[1024]{0:T(1024)S(1)} %pad_clamp_fusion), kind=kCustom, calls=%fused_computation | custom fusion | bytes 31850820 | tf_op jit(solution)/shard_map/jit(_take)/gather | solution.py:25
  117.2 10.4 %fusion.4 = f32[3,192,512]{2,1,0:T(8,128)S(1)} fusion(bf16[3,27,192,192]{3,2,1,0:T(8,128)(2,1)} %reshape.52, bf16[3,27,192,512]{3,2,1,0:T(8,128)(2,1)} %bitcast.17, pred[3,27]{1,0:T(4,128)(4,1)S(1)} %get-tuple-element.7), kind=kOutput, calls=%fused_computation.6 | convolution fusion | flops 3065610240 | bytes 23076944 | tf_op jit(solution)/shard_map/bkrc,bkcp->brp/dot_general | solution.py:27
  127.6 0.9 copy.8
  128.5 29.8 %all_to_all.4 = f32[3,192,512]{1,0,2:T(4,128)S(1)} all-to-all(f32[3,192,512]{1,0,2:T(4,128)S(1)} %copy.8), channel_id=1, replica_groups=mesh['slab'=64,'grp'=4] {'grp'}, dimensions={2} | all-to-all | bytes 2359296 | tf_op jit(solution)/shard_map/all_to_all | solution.py:41
  158.3 0.5 broadcast_multiply_fusion
  158.8 0.7 copy.9
  159.5 3.1 multiply_reduce_fusion.1
  162.6 158.1 %all-reduce = (f32[1,128]{1,0:T(1,128)S(1)}, f32[1,128]{1,0:T(1,128)S(1)}) all-reduce(f32[1,128]{1,0:T(1,128)S(1)} %bitcast.20, f32[1,128]{1,0:T(1,128)S(1)} %bitcast.19), channel_id=1, replica_groups=mesh['slab'=64,'grp'=4] {'slab'}, use_global_device_ids=true, to_apply=%region_3.4 | all-reduce | flops 256 | bytes 2048 | tf_op jit(solution)/shard_map/psum | solution.py:45
  320.7 0.6 maximum_multiply_fusion
  (3 shorter events, 0.0 us)
Async XLA Ops:
  7.2 34.8 %all-gather.2.cloned.1.call-start = ((), (), s32[]{:S(2)}) async-start(), calls=%async_computation.1 | async-start | bytes 2949120 | tf_op jit(solution)/shard_map/all_gather | solution.py:38
  42.0 57.9 %collective-permute-start = (bf16[12,192,512]{2,1,0:T(8,128)(2,1)}, bf16[12,192,512]{2,1,0:T(8,128)(2,1)}, u32[]{:S(2)}, u32[]{:S(2)}) collective-permute-start(bf16[12,192,512]{2,1,0:T(8,128)(2,1)} %all-gather.2.cloned.1.call-done), channel_id=1, source_target_pairs={{0,4},{4,8},{8,12},{12,16},{16,20},{20,24},{24,28},{28,32},{32,36}... | collective-permute-start | bytes 7077896 | tf_op jit(solution)/shard_map/ppermute | solution.py:16
  43.6 56.4 %collective-permute-start.1 = (bf16[12,192,512]{2,1,0:T(8,128)(2,1)}, bf16[12,192,512]{2,1,0:T(8,128)(2,1)}, u32[]{:S(2)}, u32[]{:S(2)}) collective-permute-start(bf16[12,192,512]{2,1,0:T(8,128)(2,1)} %all-gather.2.cloned.1.call-done), channel_id=1, source_target_pairs={{4,0},{8,4},{12,8},{16,12},{20,16},{24,20},{28,24},{32,28},{36,32}... | collective-permute-start | bytes 7077896 | tf_op jit(solution)/shard_map/ppermute | solution.py:17
  49.8 50.2 %copy-start = (bf16[12,192,512]{2,1,0:T(8,128)(2,1)S(1)}, bf16[12,192,512]{2,1,0:T(8,128)(2,1)}, u32[]{:S(2)}) copy-start(bf16[12,192,512]{2,1,0:T(8,128)(2,1)} %all-gather.2.cloned.1.call-done) | copy-start | bytes 7077892
Sparse Core Ops, SparseCore 0:
  9.8 32.1 all-gather.1
where the time goes:
time: 329 us; the launch traced here: 328 us
  blocking collectives  188 us (57%)
  waiting for transfers between devices  72.7 us (22%)
  local copies, waits for them, and re-layouts  25.3 us (8%)
  between operations  14.1 us (4%)
  other arithmetic  11.5 us (3%)
  matrix products  10.4 us (3%)
  starting transfers between devices  6.28 us (2%)
    psum x1, blocking collectives, shards(): first, second = lax.psum((first, second), 'slab')  158 us
    ppermute x1, waiting for transfers between devices, with_halo(): before = lax.ppermute(last, axis, up)  37.9 us
    all_gather x1, waiting for transfers between devices, shards(): whole = lax.all_gather(t_cur, 'grp', axis=2, tiled=True)  34.1 us
    all_to_all x1, blocking collectives, shards(): lax.all_to_all(rows_image, 'grp', split_axis=2, concat_axis=0, tiled=True)  29.8 us
    reshape x1, local copies, waits for them, and re-layouts, apply_rows(): squares = tile_rows.reshape(tile_rows.shape[:2] + (width, width))  12.2 us
    gather x1, local copies, waits for them, and re-layouts, apply_rows(): near = jnp.take(padded, locals_rows.reshape(-1), axis=0)  11.3 us
    dot_general x1, matrix products, apply_rows(): jnp.einsum('bkrc,bkcp->brp', squares, near, preferred_element_type=jnp.fl...  10.4 us
  transfers between devices with their start and end apart: 3, of which 2 were waited for; matrix products, arithmetic and copies ran while one was open for 4% of the time, Pallas kernels for 0%

commit v1 on v0

v1 whole, which is shorter than its diff:
```python
import functools
import math

import jax
import jax.numpy as jnp
from jax import lax
from jax.experimental import pallas as pl
from jax.experimental.pallas import tpu as pltpu
from jax.sharding import PartitionSpec as P

MESH = pl.DeviceIdType.MESH
BPS, BS, NB = 12, 192, 27
MINE = 3
COLS = 128
LANES = 128
FLAT = BS * BS // LANES
PITCH = FLAT + 1
KPAD = 5248
CHUNKS = 4
CB = BPS // CHUNKS
SLABS, ZS = 64, 8


class Sems:
    def __init__(self):
        self.n = 0

    def take(self, *dims):
        size = math.prod(dims) if dims else 1
        start = self.n
        self.n += size
        return start


RX = Sems()
EX, OWN, EXC = RX.take(CHUNKS), RX.take(), RX.take(CHUNKS)
NEAR, FAR, NEARC, FARC = [RX.take(2, CHUNKS) for _ in range(4)]
IMG, M1, M2 = RX.take(3), RX.take(8), RX.take(8)
NSEM = RX.n


def relayout(x, stage, a, b, part, parts):
    per = FLAT // parts
    step = 12

    def spread(m, carry):
        for u in range(step):
            j = part * per + m * step + u
            v = x[b, :, pl.ds(pl.multiple_of(j * LANES, LANES), LANES)]
            stage[pl.ds(j, NB, stride=PITCH), :] = v.astype(jnp.float32)
        return carry

    lax.fori_loop(0, per // step, spread, 0)


def assemble(stage, a, b):
    low = lax.broadcasted_iota(jnp.int32, (BS // 2, LANES), 1) < 64
    load = lambda k, i: stage[pl.ds(k * PITCH + i, BS // 2, stride=3), :]
    turn = lambda v: pltpu.roll(v, 64, 1)

    def pair(p, last):
        k = 2 * p
        e0, e1, e2 = [load(k, i) for i in range(3)]
        if last:
            zero = jnp.zeros_like(e0)
            f1, f2, rf0, rf1 = zero, zero, zero, zero
        else:
            f0, f1, f2 = [load(k + 1, i) for i in range(3)]
            rf0, rf1 = turn(f0), turn(f1)
        re1, re2 = turn(e1), turn(e2)
        even = [e0, jnp.where(low, e1, rf0), jnp.where(low, rf0, rf1)]
        odd = [jnp.where(low, re1, re2), jnp.where(low, re2, f1), f2]
        for t in range(2 if last else 3):
            at = pl.ds(pl.multiple_of(p * 384 + 128 * t, 128), LANES)
            a[b, 0 : BS // 2, at] = even[t].astype(jnp.bfloat16)
            a[b, BS // 2 : BS, at] = odd[t].astype(jnp.bfloat16)

    def body(p, carry):
        pair(p, False)
        return carry

    lax.fori_loop(0, NB // 2, body, 0)
    pair(NB // 2, True)


def multiply(ids, a, near, out):
    def one(b, carry):
        def rhs(k):
            n = ids[b * NB + k]
            return jnp.concatenate([near[0, n], near[1, n]], axis=1)

        total = None
        for first in range(0, NB, 4):
            ks = range(first, min(first + 4, NB))
            parts = [rhs(k) for k in ks]
            if len(parts) == 3:
                parts.append(jnp.zeros((64, 2 * COLS), jnp.bfloat16))
            right = jnp.concatenate(parts, axis=0)
            left = a[b, :, first * BS : first * BS + right.shape[0]]
            term = jnp.dot(left, right, preferred_element_type=jnp.float32)
            total = term if total is None else total + term
        half = BS // 2
        for e in range(2):
            for c in range(2):
                out[c, b, pl.ds(e, half, stride=2), :] = total[
                    half * e : half * (e + 1), COLS * c : COLS * (c + 1)
                ]
        return carry

    lax.fori_loop(0, MINE, one, 0)


def kernel(
    neighbours, tiles, t_cur, t_prev, probes, t_next, moments,
    x, stage, a, near, far, out_far, out_near, image, prev, probe, ids, sums1, sums2,
    local, ssem, rsem,
):
    s, g = lax.axis_index("slab"), lax.axis_index("grp")
    z = lax.rem(s, ZS)
    row = lax.div(s, ZS)
    h, c = lax.div(g, 2), lax.rem(g, 2)
    up, down = lax.rem(s + 1, SLABS), lax.rem(s + SLABS - 1, SLABS)
    here = lambda hh, cc: (s, hh * 2 + cc)
    partner, across, cross = here(h, 1 - c), here(1 - h, c), here(1 - h, 1 - c)
    zpeer = lambda o: (row * ZS + lax.rem(z + o, ZS), g)
    rpeer = lambda o: (lax.rem(row + o, 8) * ZS + z, g)
    sides = (up, down)
    edge = (z == ZS - 1, z == 0)
    other = (1 - h) * 2 + c

    loads = [
        pltpu.make_async_copy(t_cur, near.at[c, pl.ds(BPS, BPS)], local.at[0]),
        pltpu.make_async_copy(t_prev, prev, local.at[1]),
        pltpu.make_async_copy(probes, probe, local.at[2]),
    ] + [pltpu.make_async_copy(tiles.at[b], x.at[b], local.at[3 + b]) for b in range(MINE)]

    barrier = pltpu.get_barrier_semaphore()
    peers = [partner, across, cross]
    peers += [(side, g) for side in sides] + [(side, other) for side in sides]
    peers += [zpeer(o) for o in range(1, ZS)] + [rpeer(o) for o in range(1, 8)]
    for peer in peers:
        pl.semaphore_signal(barrier, 1, device_id=peer, device_id_type=MESH)
    for load in loads:
        load.start()

    def indices(b, carry):
        for k in range(NB):
            n = neighbours[g * MINE + b, k]
            rel = lax.rem(lax.div(n, BPS) - s + 1 + SLABS, SLABS)
            ids[b * NB + k] = jnp.minimum(rel, 2) * BPS + lax.rem(n, BPS)
        return carry

    lax.fori_loop(0, MINE, indices, 0)
    pl.semaphore_wait(barrier, len(peers))

    def send(src, dst, sem, device):
        return pltpu.make_async_remote_copy(
            src, dst, ssem.at[sem], rsem.at[sem], device_id=device, device_id_type=MESH
        )

    def mine(i):
        return t_cur.at[pl.ds(i * CB, CB)]

    def slot(buf, col, d, i):
        return buf.at[col, pl.ds(d * BPS + i * CB, CB)]

    def exchange(i):
        return send(mine(i), slot(far, c, 1, i), EX + i, across)

    def near_halo(d, i):
        return send(mine(i), slot(near, c, 2 * d, i), NEAR + d * CHUNKS + i, (sides[d], g))

    def far_direct(d, i):
        return send(mine(i), slot(far, c, 2 * d, i), FAR + d * CHUNKS + i, (sides[d], other))

    def far_relay(d, i):
        return send(slot(far, c, 1, i), slot(far, c, 2 * d, i), FAR + d * CHUNKS + i, (sides[d], g))

    def to_partner(buf, d, i, sem):
        return send(slot(buf, c, d, i), slot(buf, c, d, i), sem, partner)

    own_copy = send(t_cur, near.at[c, pl.ds(BPS, BPS)], OWN, partner)

    for i in range(CHUNKS):
        exchange(i).start()
    for d in range(2):
        near_halo(d, 0).start()
    for d in range(2):
        @pl.when(edge[d])
        def _():
            for i in range(CHUNKS):
                far_direct(d, i).start()
    own_copy.start()

    for i in range(CHUNKS):
        exchange(i).wait_recv()
        for d in range(2):
            @pl.when(jnp.logical_not(edge[d]))
            def _():
                far_relay(d, i).start()
        to_partner(far, 1, i, EXC + i).start()
        if i == CHUNKS - 1:
            for d in range(2):
                for j in range(1, CHUNKS):
                    near_halo(d, j).start()
        if i < MINE:
            loads[3 + i].wait()
            relayout(x, stage, a, i, 0, 1)
            assemble(stage, a, i)

    for i in range(CHUNKS):
        for d in range(2):
            far_relay(d, i).wait_recv()
            to_partner(far, 2 * d, i, FARC + d * CHUNKS + i).start()
    for i in range(CHUNKS):
        to_partner(far, 1, i, EXC + i).wait_recv()
        for d in range(2):
            to_partner(far, 2 * d, i, FARC + d * CHUNKS + i).wait_recv()

    multiply(ids, a, far, out_far)

    def far_image(r):
        col = lax.rem(c + r, 2)
        return send(out_far.at[col], image.at[pl.ds(g * MINE, MINE)], IMG + 1 + r, here(1 - h, col))

    for r in range(2):
        far_image(r).start()

    for i in range(CHUNKS):
        for d in range(2):
            near_halo(d, i).wait_recv()
            to_partner(near, 2 * d, i, NEARC + d * CHUNKS + i).start()
    loads[0].wait()
    own_copy.wait_recv()
    for i in range(CHUNKS):
        for d in range(2):
            to_partner(near, 2 * d, i, NEARC + d * CHUNKS + i).wait_recv()

    multiply(ids, a, near, out_near)

    near_image = send(out_near.at[1 - c], image.at[pl.ds(g * MINE, MINE)], IMG, partner)
    near_image.start()

    loads[1].wait()
    loads[2].wait()

    def finish(first, source, at, sums):
        def body(b, sums):
            blk = first + b
            value = 2.0 * source[at + b] - prev[blk]
            t_next[blk] = value
            fold = lambda v: jnp.sum(v.reshape(BS // 8, 8, COLS), axis=0)
            return (
                sums[0] + fold(probe[blk] * value),
                sums[1] + fold(near[c, BPS + blk].astype(jnp.float32) * value),
            )

        return lax.fori_loop(0, MINE, body, sums)

    zero = jnp.zeros((8, COLS), jnp.float32)
    sums = finish(g * MINE, out_near.at[c], 0, (zero, zero))
    near_image.wait_recv()
    first = (h * 2 + 1 - c) * MINE
    sums = finish(first, image, first, sums)
    for r in range(2):
        far_image(r).wait_recv()
        first = ((1 - h) * 2 + lax.rem(c + r, 2)) * MINE
        sums = finish(first, image, first, sums)

    top = lax.broadcasted_iota(jnp.int32, (8, COLS), 0)
    pack = lambda p, q: jnp.where(
        top == 0, jnp.sum(p, axis=0, keepdims=True), jnp.where(top == 1, jnp.sum(q, axis=0, keepdims=True), 0.0)
    )

    def spread(buf, me, peer, sem, value):
        buf[me] = value
        copies = [send(buf.at[me], buf.at[me], sem + o, peer(o)) for o in range(1, 8)]
        for copy in copies:
            copy.start()
        for copy in copies:
            copy.wait_recv()
        total = buf[0]
        for i in range(1, 8):
            total = total + buf[i]
        return total, copies

    part, copies1 = spread(sums1, z, zpeer, M1, pack(*sums))
    whole, copies2 = spread(sums2, row, rpeer, M2, part)
    factor = 1.0 / math.sqrt(SLABS * BPS * BS)
    moments[...] = whole[0:2] * factor

    own_copy.wait_send()
    near_image.wait_send()
    for r in range(2):
        far_image(r).wait_send()
    for i in range(CHUNKS):
        exchange(i).wait_send()
        to_partner(far, 1, i, EXC + i).wait_send()
        for d in range(2):
            near_halo(d, i).wait_send()
            far_relay(d, i).wait_send()
            to_partner(far, 2 * d, i, FARC + d * CHUNKS + i).wait_send()
            to_partner(near, 2 * d, i, NEARC + d * CHUNKS + i).wait_send()
    for copy in copies1 + copies2:
        copy.wait_send()


def shards(tiles, neighbours, t_cur, t_prev, probes):
    f32, bf16 = jnp.float32, jnp.bfloat16
    anywhere = pl.BlockSpec(memory_space=pl.ANY)
    vmem = pl.BlockSpec(memory_space=pltpu.VMEM)
    return pl.pallas_call(
        kernel,
        out_shape=(
            jax.ShapeDtypeStruct((BPS, BS, COLS), f32),
            jax.ShapeDtypeStruct((2, COLS), f32),
        ),
        in_specs=[pl.BlockSpec(memory_space=pltpu.SMEM)] + [anywhere] * 4,
        out_specs=(vmem, vmem),
        scratch_shapes=[
            pltpu.VMEM((MINE, NB, BS * BS), bf16),
            pltpu.VMEM((NB * PITCH, LANES), f32),
            pltpu.VMEM((MINE, BS, KPAD), bf16),
            pltpu.VMEM((2, 3 * BPS, BS, COLS), bf16),
            pltpu.VMEM((2, 3 * BPS, BS, COLS), bf16),
            pltpu.VMEM((2, MINE, BS, COLS), f32),
            pltpu.VMEM((2, MINE, BS, COLS), f32),
            pltpu.VMEM((BPS, BS, COLS), f32),
            pltpu.VMEM((BPS, BS, COLS), f32),
            pltpu.VMEM((BPS, BS, COLS), f32),
            pltpu.SMEM((MINE * NB,), jnp.int32),
            pltpu.VMEM((8, 8, COLS), f32),
            pltpu.VMEM((8, 8, COLS), f32),
            pltpu.SemaphoreType.DMA((6,)),
            pltpu.SemaphoreType.DMA((NSEM,)),
            pltpu.SemaphoreType.DMA((NSEM,)),
        ],
        compiler_params=pltpu.CompilerParams(
            collective_id=0, has_side_effects=True, vmem_limit_bytes=60 << 20
        ),
        name="chebyshev_step",
    )(neighbours, tiles, t_cur, t_prev, probes)


def solution(mesh):
    placed = (
        P(("slab", "grp"), None, None),
        P("slab", None),
        P("slab", None, "grp"),
        P("slab", None, "grp"),
        P("slab", None, "grp"),
    )
    return jax.shard_map(
        shards,
        mesh=mesh,
        in_specs=placed,
        out_specs=(P("slab", None, "grp"), P(None, "grp")),
        check_vma=False,
    )
```

time: 329 us -> 84.5 us (0.26)
  the two profiles are of different devices: /device:TPU:0 before, /device:TPU:6 now
where the time goes in v1:
time: 84.5 us; the launch traced here: 84.3 us
  Pallas kernels  80.7 us (96%)
  local copies, waits for them, and re-layouts  2.93 us (3%)
    pallas_call x1, Pallas kernels, shards(): pl.pallas_call(kernel, out_shape=(jax.ShapeDtypeStruct((BPS, BS, COLS), f...  80.7 us
    unnamed x4, local copies, waits for them, and re-layouts  2.93 us

profile of v1, /device:TPU:6, one launch (start us, length us, event | category | flops | bytes accessed | tf_op | source)
XLA Modules:
  0.0 84.3 jit_solution(9387147911192254176)
XLA Ops:
  0.6 80.7 %chebyshev_step.1 = (f32[12,192,128]{2,1,0:T(8,128)}, f32[2,128]{1,0:T(2,128)}) custom-call(s32[12,27]{1,0:T(8,128)} %neighbours.1, bf16[3,27,36864]{2,1,0:T(8,128)(2,1)} %tiles.1, bf16[12,192,128]{2,1,0:T(8,128)(2,1)} %t_cur.1, f32[12,192,128]{2,1,0:T(8,128)} %t_prev.1, f32[12,192,128]{2,1,0:T(8,128)} %probes.1), custom_call_target="tpu_custom_call" | custom-call | tf_op jit(solution)/shard_map/chebyshev_step/pallas_call | solution.py:312
  81.4 0.0 copy-start
  81.4 2.4 %copy.9 = f32[12,192,128]{2,1,0:T(8,128)} copy(f32[12,192,128]{2,1,0:T(8,128)} %get-tuple-element.4) | data formatting | bytes 2359296
  83.7 0.0 copy-done
  83.7 0.6 copy.10
Async XLA Ops:
  81.4 2.4 %copy-start = (f32[2,128]{1,0:T(2,128)S(1)}, f32[2,128]{1,0:T(2,128)}, u32[]{:S(2)}) copy-start(f32[2,128]{1,0:T(2,128)} %get-tuple-element.5) | copy-start | bytes 3076

commit v2 on v1

--- a/solution.py
+++ b/solution.py
@@ -16,7 +16,9 @@
 FLAT = BS * BS // LANES
 PITCH = FLAT + 1
 KPAD = 5248
-CHUNKS = 4
+CHUNKS = 6
+AHEAD = 2
+EARLY = 3
 CB = BPS // CHUNKS
 SLABS, ZS = 64, 8
 
@@ -34,23 +36,22 @@
 
 RX = Sems()
 EX, OWN, EXC = RX.take(CHUNKS), RX.take(), RX.take(CHUNKS)
-NEAR, FAR, NEARC, FARC = [RX.take(2, CHUNKS) for _ in range(4)]
-IMG, M1, M2 = RX.take(3), RX.take(8), RX.take(8)
+NEAR, FAR, NEARC, FARC, XS = [RX.take(2, CHUNKS) for _ in range(5)]
+IMG, IMGF, M1, M2 = RX.take(), RX.take(2, MINE), RX.take(8), RX.take(8)
 NSEM = RX.n
 
 
-def relayout(x, stage, a, b, part, parts):
-    per = FLAT // parts
+def relayout(x, stage, b):
     step = 12
 
     def spread(m, carry):
         for u in range(step):
-            j = part * per + m * step + u
+            j = m * step + u
             v = x[b, :, pl.ds(pl.multiple_of(j * LANES, LANES), LANES)]
             stage[pl.ds(j, NB, stride=PITCH), :] = v.astype(jnp.float32)
         return carry
 
-    lax.fori_loop(0, per // step, spread, 0)
+    lax.fori_loop(0, FLAT // step, spread, 0)
 
 
 def assemble(stage, a, b):
@@ -83,7 +84,7 @@
     pair(NB // 2, True)
 
 
-def multiply(ids, a, near, out):
+def multiply(ids, a, near, out, after=None):
     def one(b, carry):
         def rhs(k):
             n = ids[b * NB + k]
@@ -105,6 +106,8 @@
                 out[c, b, pl.ds(e, half, stride=2), :] = total[
                     half * e : half * (e + 1), COLS * c : COLS * (c + 1)
                 ]
+        if after is not None:
+            after(b)
         return carry
 
     lax.fori_loop(0, MINE, one, 0)
@@ -112,7 +115,7 @@
 
 def kernel(
     neighbours, tiles, t_cur, t_prev, probes, t_next, moments,
-    x, stage, a, near, far, out_far, out_near, image, prev, probe, ids, sums1, sums2,
+    x, stage, a, near, far, out_far, out_near, image, passing, prev, probe, ids, sums1, sums2,
     local, ssem, rsem,
 ):
     s, g = lax.axis_index("slab"), lax.axis_index("grp")
@@ -124,9 +127,17 @@
     partner, across, cross = here(h, 1 - c), here(1 - h, c), here(1 - h, 1 - c)
     zpeer = lambda o: (row * ZS + lax.rem(z + o, ZS), g)
     rpeer = lambda o: (lax.rem(row + o, 8) * ZS + z, g)
+    other = (1 - h) * 2 + c
+    beside = lambda slab: slab + ZS - 2 * ZS * lax.rem(lax.div(slab, ZS), 2)
+    sx = beside(s)
+    xpeer = ((sx, g), (sx, other))
     sides = (up, down)
     edge = (z == ZS - 1, z == 0)
-    other = (1 - h) * 2 + c
+    on_edge = jnp.logical_or(edge[0], edge[1])
+    inner = [jnp.logical_not(e) for e in edge]
+    de = jnp.where(edge[1], 1, 0)
+    beyond = (lax.rem(jnp.where(edge[1], sx + SLABS - 1, sx + 1), SLABS), g)
+    greet = [(jnp.where(edge[d], beside(sides[d]), sides[d]), g) for d in range(2)]
 
     loads = [
         pltpu.make_async_copy(t_cur, near.at[c, pl.ds(BPS, BPS)], local.at[0]),
@@ -136,7 +147,7 @@
 
     barrier = pltpu.get_barrier_semaphore()
     peers = [partner, across, cross]
-    peers += [(side, g) for side in sides] + [(side, other) for side in sides]
+    peers += greet + list(xpeer)
     peers += [zpeer(o) for o in range(1, ZS)] + [rpeer(o) for o in range(1, 8)]
     for peer in peers:
         pl.semaphore_signal(barrier, 1, device_id=peer, device_id_type=MESH)
@@ -170,8 +181,18 @@
     def near_halo(d, i):
         return send(mine(i), slot(near, c, 2 * d, i), NEAR + d * CHUNKS + i, (sides[d], g))
 
-    def far_direct(d, i):
-        return send(mine(i), slot(far, c, 2 * d, i), FAR + d * CHUNKS + i, (sides[d], other))
+    def chunk(e, i):
+        return passing.at[e, pl.ds(i * CB, CB)]
+
+    def hand(e, i):
+        return send(mine(i), chunk(e, i), XS + e * CHUNKS + i, xpeer[e])
+
+    def forward(e, i):
+        base = (NEAR, FAR)[e] + de * CHUNKS + i
+        return send(chunk(e, i), slot((near, far)[e], c, 2 * de, i), base, beyond)
+
+    def forward_across(i):
+        return send(chunk(i % 2, i), slot(far, c, 1, i), EX + i, xpeer[1 - i % 2])
 
     def far_relay(d, i):
         return send(slot(far, c, 1, i), slot(far, c, 2 * d, i), FAR + d * CHUNKS + i, (sides[d], g))
@@ -181,32 +202,51 @@
 
     own_copy = send(t_cur, near.at[c, pl.ds(BPS, BPS)], OWN, partner)
 
-    for i in range(CHUNKS):
-        exchange(i).start()
+    @pl.when(on_edge)
+    def _():
+        for i in range(AHEAD):
+            for e in range(2):
+                hand(e, i).start()
+
+    @pl.when(jnp.logical_not(on_edge))
+    def _():
+        for i in range(CHUNKS):
+            exchange(i).start()
+
     for d in range(2):
-        near_halo(d, 0).start()
-    for d in range(2):
-        @pl.when(edge[d])
+        @pl.when(inner[d])
         def _():
-            for i in range(CHUNKS):
-                far_direct(d, i).start()
+            for i in range(EARLY):
+                near_halo(d, i).start()
     own_copy.start()
 
-    for i in range(CHUNKS):
-        exchange(i).wait_recv()
-        for d in range(2):
-            @pl.when(jnp.logical_not(edge[d]))
+    for i in range(CHUNKS + 1):
+        if i < CHUNKS:
+            @pl.when(on_edge)
             def _():
-                far_relay(d, i).start()
-        to_partner(far, 1, i, EXC + i).start()
-        if i == CHUNKS - 1:
+                for e in range(2):
+                    hand(e, i).wait_recv()
+                forward_across(i).start()
+                for e in range(2):
+                    if i + AHEAD < CHUNKS:
+                        hand(e, i + AHEAD).start()
+                    forward(e, i).start()
+
+        if i > 0:
+            j = i - 1
+            exchange(j).wait_recv()
             for d in range(2):
-                for j in range(1, CHUNKS):
-                    near_halo(d, j).start()
-        if i < MINE:
-            loads[3 + i].wait()
-            relayout(x, stage, a, i, 0, 1)
-            assemble(stage, a, i)
+                @pl.when(inner[d])
+                def _():
+                    far_relay(d, j).start()
+                    if j == CHUNKS - 1:
+                        for k in range(EARLY, CHUNKS):
+                            near_halo(d, k).start()
+            to_partner(far, 1, j, EXC + j).start()
+            if j < MINE:
+                loads[3 + j].wait()
+                relayout(x, stage, j)
+                assemble(stage, a, j)
 
     for i in range(CHUNKS):
         for d in range(2):
@@ -217,14 +257,16 @@
         for d in range(2):
             to_partner(far, 2 * d, i, FARC + d * CHUNKS + i).wait_recv()
 
-    multiply(ids, a, far, out_far)
-
-    def far_image(r):
+    def far_image(r, b):
         col = lax.rem(c + r, 2)
-        return send(out_far.at[col], image.at[pl.ds(g * MINE, MINE)], IMG + 1 + r, here(1 - h, col))
-
-    for r in range(2):
-        far_image(r).start()
+        sem = IMGF + r * MINE + b
+        return send(out_far.at[col, b], image.at[g * MINE + b], sem, here(1 - h, col))
+
+    def send_far(b):
+        for r in range(2):
+            far_image(r, b).start()
+
+    multiply(ids, a, far, out_far, send_far)
 
     for i in range(CHUNKS):
         for d in range(2):
@@ -244,7 +286,7 @@
     loads[1].wait()
     loads[2].wait()
 
-    def finish(first, source, at, sums):
+    def finish(first, source, at):
         def body(b, sums):
             blk = first + b
             value = 2.0 * source[at + b] - prev[blk]
@@ -255,17 +297,25 @@
                 sums[1] + fold(near[c, BPS + blk].astype(jnp.float32) * value),
             )
 
-        return lax.fori_loop(0, MINE, body, sums)
+        return body
+
+    def finish_all(first, source, at, sums):
+        return lax.fori_loop(0, MINE, finish(first, source, at), sums)
 
     zero = jnp.zeros((8, COLS), jnp.float32)
-    sums = finish(g * MINE, out_near.at[c], 0, (zero, zero))
+    sums = finish_all(g * MINE, out_near.at[c], 0, (zero, zero))
     near_image.wait_recv()
     first = (h * 2 + 1 - c) * MINE
-    sums = finish(first, image, first, sums)
-    for r in range(2):
-        far_image(r).wait_recv()
-        first = ((1 - h) * 2 + lax.rem(c + r, 2)) * MINE
-        sums = finish(first, image, first, sums)
+    sums = finish_all(first, image, first, sums)
+
+    def arrived(b, sums):
+        for r in range(2):
+            far_image(r, b).wait_recv()
+            first = ((1 - h) * 2 + lax.rem(c + r, 2)) * MINE
+            sums = finish(first, image, first)(b, sums)
+        return sums
+
+    sums = lax.fori_loop(0, MINE, arrived, sums)
 
     top = lax.broadcasted_iota(jnp.int32, (8, COLS), 0)
     pack = lambda p, q: jnp.where(
@@ -292,13 +342,27 @@
     own_copy.wait_send()
     near_image.wait_send()
     for r in range(2):
-        far_image(r).wait_send()
+        for b in range(MINE):
+            far_image(r, b).wait_send()
     for i in range(CHUNKS):
-        exchange(i).wait_send()
+        @pl.when(on_edge)
+        def _():
+            for e in range(2):
+                hand(e, i).wait_send()
+                forward(e, i).wait_send()
+            forward_across(i).wait_send()
+
+        @pl.when(jnp.logical_not(on_edge))
+        def _():
+            exchange(i).wait_send()
+
         to_partner(far, 1, i, EXC + i).wait_send()
         for d in range(2):
-            near_halo(d, i).wait_send()
-            far_relay(d, i).wait_send()
+            @pl.when(inner[d])
+            def _():
+                near_halo(d, i).wait_send()
+                far_relay(d, i).wait_send()
+
             to_partner(far, 2 * d, i, FARC + d * CHUNKS + i).wait_send()
             to_partner(near, 2 * d, i, NEARC + d * CHUNKS + i).wait_send()
     for copy in copies1 + copies2:
@@ -326,6 +390,7 @@
             pltpu.VMEM((2, MINE, BS, COLS), f32),
             pltpu.VMEM((2, MINE, BS, COLS), f32),
             pltpu.VMEM((BPS, BS, COLS), f32),
+            pltpu.VMEM((2, BPS, BS, COLS), bf16),
             pltpu.VMEM((BPS, BS, COLS), f32),
             pltpu.VMEM((BPS, BS, COLS), f32),
             pltpu.SMEM((MINE * NB,), jnp.int32),

time: 84.5 us -> 71.7 us (0.85)
  the two profiles are of different devices: /device:TPU:6 before, /device:TPU:1 now
where the time goes in v2:
time: 71.7 us; the launch traced here: 71.1 us
  Pallas kernels  67.5 us (94%)
  local copies, waits for them, and re-layouts  2.93 us (4%)
    pallas_call x1, Pallas kernels, shards(): pl.pallas_call(kernel, out_shape=(jax.ShapeDtypeStruct((BPS, BS, COLS), f...  67.5 us
    unnamed x4, local copies, waits for them, and re-layouts  2.93 us

profile of v2, /device:TPU:1, one launch (start us, length us, event | category | flops | bytes accessed | tf_op | source)
XLA Modules:
  0.0 71.1 jit_solution(9247143199536684950)
XLA Ops:
  0.6 67.5 %chebyshev_step.1 = (f32[12,192,128]{2,1,0:T(8,128)}, f32[2,128]{1,0:T(2,128)}) custom-call(s32[12,27]{1,0:T(8,128)} %neighbours.1, bf16[3,27,36864]{2,1,0:T(8,128)(2,1)} %tiles.1, bf16[12,192,128]{2,1,0:T(8,128)(2,1)} %t_cur.1, f32[12,192,128]{2,1,0:T(8,128)} %t_prev.1, f32[12,192,128]{2,1,0:T(8,128)} %probes.1), custom_call_target="tpu_custom_call" | custom-call | tf_op jit(solution)/shard_map/chebyshev_step/pallas_call | solution.py:376
  68.1 0.0 copy-start
  68.1 2.4 %copy.9 = f32[12,192,128]{2,1,0:T(8,128)} copy(f32[12,192,128]{2,1,0:T(8,128)} %get-tuple-element.4) | data formatting | bytes 2359296
  70.5 0.0 copy-done
  70.5 0.6 copy.10
Async XLA Ops:
  68.1 2.4 %copy-start = (f32[2,128]{1,0:T(2,128)S(1)}, f32[2,128]{1,0:T(2,128)}, u32[]{:S(2)}) copy-start(f32[2,128]{1,0:T(2,128)} %get-tuple-element.5) | copy-start | bytes 3076

commit v3 on v2

--- a/solution.py
+++ b/solution.py
@@ -17,8 +17,10 @@
 PITCH = FLAT + 1
 KPAD = 5248
 CHUNKS = 6
-AHEAD = 2
+LAG = 2
+AHEAD = 3
 EARLY = 3
+HALF = CHUNKS // 2
 CB = BPS // CHUNKS
 SLABS, ZS = 64, 8
 
@@ -35,9 +37,9 @@
 
 
 RX = Sems()
-EX, OWN, EXC = RX.take(CHUNKS), RX.take(), RX.take(CHUNKS)
+EX, OWN, EXC = RX.take(CHUNKS), RX.take(2), RX.take(CHUNKS)
 NEAR, FAR, NEARC, FARC, XS = [RX.take(2, CHUNKS) for _ in range(5)]
-IMG, IMGF, M1, M2 = RX.take(), RX.take(2, MINE), RX.take(8), RX.take(8)
+IMG, IMGF, M1, M2 = RX.take(MINE), RX.take(2, MINE), RX.take(8), RX.take(8)
 NSEM = RX.n
 
 
@@ -84,40 +86,32 @@
     pair(NB // 2, True)
 
 
-def multiply(ids, a, near, out, after=None):
+def multiply(ids, a, col, out, after):
     def one(b, carry):
-        def rhs(k):
-            n = ids[b * NB + k]
-            return jnp.concatenate([near[0, n], near[1, n]], axis=1)
-
         total = None
         for first in range(0, NB, 4):
-            ks = range(first, min(first + 4, NB))
-            parts = [rhs(k) for k in ks]
+            parts = [col[ids[b * NB + k]] for k in range(first, min(first + 4, NB))]
             if len(parts) == 3:
-                parts.append(jnp.zeros((64, 2 * COLS), jnp.bfloat16))
+                parts.append(jnp.zeros((64, COLS), jnp.bfloat16))
             right = jnp.concatenate(parts, axis=0)
             left = a[b, :, first * BS : first * BS + right.shape[0]]
             term = jnp.dot(left, right, preferred_element_type=jnp.float32)
             total = term if total is None else total + term
         half = BS // 2
         for e in range(2):
-            for c in range(2):
-                out[c, b, pl.ds(e, half, stride=2), :] = total[
-                    half * e : half * (e + 1), COLS * c : COLS * (c + 1)
-                ]
-        if after is not None:
-            after(b)
+            out[b, pl.ds(e, half, stride=2), :] = total[half * e : half * (e + 1)]
+        after(b)
         return carry
 
     lax.fori_loop(0, MINE, one, 0)
 
 
 def kernel(
-    neighbours, tiles, t_cur, t_prev, probes, t_next, moments,
-    x, stage, a, near, far, out_far, out_near, image, passing, prev, probe, ids, sums1, sums2,
+    table, tiles, t_cur, t_prev, probes, t_next, moments,
+    x, stage, a, near0, near1, far0, far1, own, out_far, out_near, image, passing, prev, probe, neighbours, ids, sums1, sums2,
     local, ssem, rsem,
 ):
+    near, far = (near0, near1), (far0, far1)
     s, g = lax.axis_index("slab"), lax.axis_index("grp")
     z = lax.rem(s, ZS)
     row = lax.div(s, ZS)
@@ -140,10 +134,11 @@
     greet = [(jnp.where(edge[d], beside(sides[d]), sides[d]), g) for d in range(2)]
 
     loads = [
-        pltpu.make_async_copy(t_cur, near.at[c, pl.ds(BPS, BPS)], local.at[0]),
+        pltpu.make_async_copy(t_cur, own, local.at[0]),
         pltpu.make_async_copy(t_prev, prev, local.at[1]),
         pltpu.make_async_copy(probes, probe, local.at[2]),
     ] + [pltpu.make_async_copy(tiles.at[b], x.at[b], local.at[3 + b]) for b in range(MINE)]
+    loads.append(pltpu.make_async_copy(table, neighbours, local.at[3 + MINE]))
 
     barrier = pltpu.get_barrier_semaphore()
     peers = [partner, across, cross]
@@ -151,6 +146,14 @@
     peers += [zpeer(o) for o in range(1, ZS)] + [rpeer(o) for o in range(1, 8)]
     for peer in peers:
         pl.semaphore_signal(barrier, 1, device_id=peer, device_id_type=MESH)
+    def place_own(k):
+        return pltpu.make_async_copy(t_cur, near[k].at[pl.ds(BPS, BPS)], local.at[4 + MINE])
+
+    for k in range(2):
+        @pl.when(c == k)
+        def _():
+            place_own(k).start()
+
     for load in loads:
         load.start()
 
@@ -161,7 +164,6 @@
             ids[b * NB + k] = jnp.minimum(rel, 2) * BPS + lax.rem(n, BPS)
         return carry
 
-    lax.fori_loop(0, MINE, indices, 0)
     pl.semaphore_wait(barrier, len(peers))
 
     def send(src, dst, sem, device):
@@ -169,17 +171,17 @@
             src, dst, ssem.at[sem], rsem.at[sem], device_id=device, device_id_type=MESH
         )
 
+    def slot(buf, d, i):
+        return buf[i // HALF].at[pl.ds(d * BPS + c * (BPS // 2) + (i % HALF) * CB, CB)]
+
     def mine(i):
-        return t_cur.at[pl.ds(i * CB, CB)]
-
-    def slot(buf, col, d, i):
-        return buf.at[col, pl.ds(d * BPS + i * CB, CB)]
+        return slot(near, 1, i)
 
     def exchange(i):
-        return send(mine(i), slot(far, c, 1, i), EX + i, across)
+        return send(mine(i), slot(far, 1, i), EX + i, across)
 
     def near_halo(d, i):
-        return send(mine(i), slot(near, c, 2 * d, i), NEAR + d * CHUNKS + i, (sides[d], g))
+        return send(mine(i), slot(near, 2 * d, i), NEAR + d * CHUNKS + i, (sides[d], g))
 
     def chunk(e, i):
         return passing.at[e, pl.ds(i * CB, CB)]
@@ -189,18 +191,38 @@
 
     def forward(e, i):
         base = (NEAR, FAR)[e] + de * CHUNKS + i
-        return send(chunk(e, i), slot((near, far)[e], c, 2 * de, i), base, beyond)
+        return send(chunk(e, i), slot((near, far)[e], 2 * de, i), base, beyond)
 
     def forward_across(i):
-        return send(chunk(i % 2, i), slot(far, c, 1, i), EX + i, xpeer[1 - i % 2])
+        return send(chunk(i % 2, i), slot(far, 1, i), EX + i, xpeer[1 - i % 2])
 
     def far_relay(d, i):
-        return send(slot(far, c, 1, i), slot(far, c, 2 * d, i), FAR + d * CHUNKS + i, (sides[d], g))
+        return send(slot(far, 1, i), slot(far, 2 * d, i), FAR + d * CHUNKS + i, (sides[d], g))
 
     def to_partner(buf, d, i, sem):
-        return send(slot(buf, c, d, i), slot(buf, c, d, i), sem, partner)
-
-    own_copy = send(t_cur, near.at[c, pl.ds(BPS, BPS)], OWN, partner)
+        return send(slot(buf, d, i), slot(buf, d, i), sem, partner)
+
+    def own_copy(p, k=0):
+        first = BPS + (BPS // 2) * (1 - c if p == 0 else c)
+        piece = near[k].at[pl.ds(first, BPS // 2)]
+        return send(piece, piece, OWN + p, partner)
+
+    place_own(0).wait()
+    for k in range(2):
+        @pl.when(c == k)
+        def _():
+            for p in range(2):
+                own_copy(p, k).start()
+
+    @pl.when(c == 1)
+    def _():
+        own_copy(0).wait_recv()
+
+    def begin(chunks):
+        @pl.when(jnp.logical_not(on_edge))
+        def _():
+            for i in chunks:
+                exchange(i).start()
 
     @pl.when(on_edge)
     def _():
@@ -208,19 +230,45 @@
             for e in range(2):
                 hand(e, i).start()
 
-    @pl.when(jnp.logical_not(on_edge))
-    def _():
-        for i in range(CHUNKS):
-            exchange(i).start()
-
+    begin(range(HALF))
     for d in range(2):
         @pl.when(inner[d])
         def _():
             for i in range(EARLY):
                 near_halo(d, i).start()
-    own_copy.start()
-
-    for i in range(CHUNKS + 1):
+
+    @pl.when(c == 0)
+    def _():
+        own_copy(0).wait_recv()
+
+    begin(range(HALF, CHUNKS))
+    loads[3 + MINE].wait()
+    lax.fori_loop(0, MINE, indices, 0)
+
+    def prepare(b):
+        loads[3 + b].wait()
+        relayout(x, stage, b)
+        assemble(stage, a, b)
+
+
+    def far_forward(col):
+        for i in range(col * HALF, (col + 1) * HALF):
+            for d in range(2):
+                far_relay(d, i).wait_recv()
+                to_partner(far, 2 * d, i, FARC + d * CHUNKS + i).start()
+
+    def far_image(col, b):
+        r = jnp.where(col == c, 0, 1)
+        return send(out_far.at[col, b], image.at[g * MINE + b], IMGF + r * MINE + b, here(1 - h, col))
+
+    def far_multiply(col):
+        for i in range(col * HALF, (col + 1) * HALF):
+            to_partner(far, 1, i, EXC + i).wait_recv()
+            for d in range(2):
+                to_partner(far, 2 * d, i, FARC + d * CHUNKS + i).wait_recv()
+        multiply(ids, a, far[col], out_far.at[col], lambda b: far_image(col, b).start())
+
+    for i in range(CHUNKS + LAG):
         if i < CHUNKS:
             @pl.when(on_edge)
             def _():
@@ -232,59 +280,55 @@
                         hand(e, i + AHEAD).start()
                     forward(e, i).start()
 
-        if i > 0:
-            j = i - 1
+        if i >= LAG:
+            j = i - LAG
             exchange(j).wait_recv()
             for d in range(2):
                 @pl.when(inner[d])
                 def _():
                     far_relay(d, j).start()
+                    @pl.when(on_edge)
+                    def _():
+                        if j + EARLY < CHUNKS:
+                            near_halo(d, j + EARLY).start()
+
                     if j == CHUNKS - 1:
-                        for k in range(EARLY, CHUNKS):
-                            near_halo(d, k).start()
+                        @pl.when(jnp.logical_not(on_edge))
+                        def _():
+                            for k in range(EARLY, CHUNKS):
+                                near_halo(d, k).start()
             to_partner(far, 1, j, EXC + j).start()
             if j < MINE:
-                loads[3 + j].wait()
-                relayout(x, stage, j)
-                assemble(stage, a, j)
-
-    for i in range(CHUNKS):
-        for d in range(2):
-            far_relay(d, i).wait_recv()
-            to_partner(far, 2 * d, i, FARC + d * CHUNKS + i).start()
-    for i in range(CHUNKS):
-        to_partner(far, 1, i, EXC + i).wait_recv()
-        for d in range(2):
-            to_partner(far, 2 * d, i, FARC + d * CHUNKS + i).wait_recv()
-
-    def far_image(r, b):
-        col = lax.rem(c + r, 2)
-        sem = IMGF + r * MINE + b
-        return send(out_far.at[col, b], image.at[g * MINE + b], sem, here(1 - h, col))
-
-    def send_far(b):
-        for r in range(2):
-            far_image(r, b).start()
-
-    multiply(ids, a, far, out_far, send_far)
-
-    for i in range(CHUNKS):
-        for d in range(2):
-            near_halo(d, i).wait_recv()
-            to_partner(near, 2 * d, i, NEARC + d * CHUNKS + i).start()
-    loads[0].wait()
-    own_copy.wait_recv()
-    for i in range(CHUNKS):
-        for d in range(2):
-            to_partner(near, 2 * d, i, NEARC + d * CHUNKS + i).wait_recv()
-
-    multiply(ids, a, near, out_near)
-
-    near_image = send(out_near.at[1 - c], image.at[pl.ds(g * MINE, MINE)], IMG, partner)
-    near_image.start()
-
-    loads[1].wait()
-    loads[2].wait()
+                prepare(j)
+            if j == CHUNKS - 2:
+                far_forward(0)
+
+    far_multiply(0)
+    far_forward(1)
+    far_multiply(1)
+
+    def near_image(b):
+        return send(out_near.at[1 - c, b], image.at[g * MINE + b], IMG + b, partner)
+
+    own_copy(1).wait_recv()
+    for col in range(2):
+        for i in range(col * HALF, (col + 1) * HALF):
+            for d in range(2):
+                near_halo(d, i).wait_recv()
+                to_partner(near, 2 * d, i, NEARC + d * CHUNKS + i).start()
+        for i in range(col * HALF, (col + 1) * HALF):
+            for d in range(2):
+                to_partner(near, 2 * d, i, NEARC + d * CHUNKS + i).wait_recv()
+
+        def after(b):
+            @pl.when(c != col)
+            def _():
+                near_image(b).start()
+
+        multiply(ids, a, near[col], out_near.at[col], after)
+
+    for k in range(3):
+        loads[k].wait()
 
     def finish(first, source, at):
         def body(b, sums):
@@ -294,7 +338,7 @@
             fold = lambda v: jnp.sum(v.reshape(BS // 8, 8, COLS), axis=0)
             return (
                 sums[0] + fold(probe[blk] * value),
-                sums[1] + fold(near[c, BPS + blk].astype(jnp.float32) * value),
+                sums[1] + fold(own[blk].astype(jnp.float32) * value),
             )
 
         return body
@@ -304,14 +348,15 @@
 
     zero = jnp.zeros((8, COLS), jnp.float32)
     sums = finish_all(g * MINE, out_near.at[c], 0, (zero, zero))
-    near_image.wait_recv()
     first = (h * 2 + 1 - c) * MINE
+    for b in range(MINE):
+        near_image(b).wait_recv()
     sums = finish_all(first, image, first, sums)
 
     def arrived(b, sums):
         for r in range(2):
-            far_image(r, b).wait_recv()
-            first = ((1 - h) * 2 + lax.rem(c + r, 2)) * MINE
+            send(out_far.at[0, b], image.at[b], IMGF + r * MINE + b, across).wait_recv()
+            first = ((1 - h) * 2 + (c if r == 0 else 1 - c)) * MINE
             sums = finish(first, image, first)(b, sums)
         return sums
 
@@ -339,11 +384,12 @@
     factor = 1.0 / math.sqrt(SLABS * BPS * BS)
     moments[...] = whole[0:2] * factor
 
-    own_copy.wait_send()
-    near_image.wait_send()
-    for r in range(2):
-        for b in range(MINE):
-            far_image(r, b).wait_send()
+    for p in range(2):
+        own_copy(p).wait_send()
+    for b in range(MINE):
+        near_image(b).wait_send()
+        for col in range(2):
+            far_image(col, b).wait_send()
     for i in range(CHUNKS):
         @pl.when(on_edge)
         def _():
@@ -379,24 +425,25 @@
             jax.ShapeDtypeStruct((BPS, BS, COLS), f32),
             jax.ShapeDtypeStruct((2, COLS), f32),
         ),
-        in_specs=[pl.BlockSpec(memory_space=pltpu.SMEM)] + [anywhere] * 4,
+        in_specs=[anywhere] * 5,
         out_specs=(vmem, vmem),
         scratch_shapes=[
             pltpu.VMEM((MINE, NB, BS * BS), bf16),
             pltpu.VMEM((NB * PITCH, LANES), f32),
             pltpu.VMEM((MINE, BS, KPAD), bf16),
-            pltpu.VMEM((2, 3 * BPS, BS, COLS), bf16),
-            pltpu.VMEM((2, 3 * BPS, BS, COLS), bf16),
+            *[pltpu.VMEM((3 * BPS, BS, COLS), bf16)] * 4,
+            pltpu.VMEM((BPS, BS, COLS), bf16),
             pltpu.VMEM((2, MINE, BS, COLS), f32),
             pltpu.VMEM((2, MINE, BS, COLS), f32),
             pltpu.VMEM((BPS, BS, COLS), f32),
             pltpu.VMEM((2, BPS, BS, COLS), bf16),
             pltpu.VMEM((BPS, BS, COLS), f32),
             pltpu.VMEM((BPS, BS, COLS), f32),
+            pltpu.SMEM((BPS, NB), jnp.int32),
             pltpu.SMEM((MINE * NB,), jnp.int32),
             pltpu.VMEM((8, 8, COLS), f32),
             pltpu.VMEM((8, 8, COLS), f32),
-            pltpu.SemaphoreType.DMA((6,)),
+            pltpu.SemaphoreType.DMA((5 + MINE,)),
             pltpu.SemaphoreType.DMA((NSEM,)),
             pltpu.SemaphoreType.DMA((NSEM,)),
         ],

time: 71.7 us -> 67.9 us (0.947)
  Pallas kernels: 67.5 us -> 64.2 us
    pallas_call x1, Pallas kernels: 67.5 us -> 64.2 us  [shards(): pl.pallas_call(kernel, out_shape=(jax.ShapeDtypeStruct((BPS, BS, COLS), f...]
where the time goes in v3:
time: 67.9 us; the launch traced here: 67.8 us
  Pallas kernels  64.2 us (95%)
  local copies, waits for them, and re-layouts  2.93 us (4%)
    pallas_call x1, Pallas kernels, shards(): pl.pallas_call(kernel, out_shape=(jax.ShapeDtypeStruct((BPS, BS, COLS), f...  64.2 us
    unnamed x4, local copies, waits for them, and re-layouts  2.93 us

profile of v3, /device:TPU:1, one launch (start us, length us, event | category | flops | bytes accessed | tf_op | source)
XLA Modules:
  0.0 67.8 jit_solution(17164234553934663026)
XLA Ops:
  0.6 64.2 %chebyshev_step.1 = (f32[12,192,128]{2,1,0:T(8,128)}, f32[2,128]{1,0:T(2,128)}) custom-call(s32[12,27]{1,0:T(8,128)} %table.1, bf16[3,27,36864]{2,1,0:T(8,128)(2,1)} %tiles.1, bf16[12,192,128]{2,1,0:T(8,128)(2,1)} %t_cur.1, f32[12,192,128]{2,1,0:T(8,128)} %t_prev.1, f32[12,192,128]{2,1,0:T(8,128)} %probes.1), custom_call_target="tpu_custom_call" | custom-call | tf_op jit(solution)/shard_map/chebyshev_step/pallas_call | solution.py:422
  64.9 0.0 copy-start
  64.9 2.4 %copy.9 = f32[12,192,128]{2,1,0:T(8,128)} copy(f32[12,192,128]{2,1,0:T(8,128)} %get-tuple-element.4) | data formatting | bytes 2359296
  67.2 0.0 copy-done
  67.2 0.6 copy.10
Async XLA Ops:
  64.9 2.4 %copy-start = (f32[2,128]{1,0:T(2,128)S(1)}, f32[2,128]{1,0:T(2,128)}, u32[]{:S(2)}) copy-start(f32[2,128]{1,0:T(2,128)} %get-tuple-element.5) | copy-start | bytes 3076

commit v4 on v3

--- a/solution.py
+++ b/solution.py
@@ -268,6 +268,29 @@
                 to_partner(far, 2 * d, i, FARC + d * CHUNKS + i).wait_recv()
         multiply(ids, a, far[col], out_far.at[col], lambda b: far_image(col, b).start())
 
+    def near_image(b):
+        return send(out_near.at[1 - c, b], image.at[g * MINE + b], IMG + b, partner)
+
+    def near_forward(col):
+        for i in range(col * HALF, (col + 1) * HALF):
+            for d in range(2):
+                near_halo(d, i).wait_recv()
+                to_partner(near, 2 * d, i, NEARC + d * CHUNKS + i).start()
+
+    def near_multiply(col):
+        if col == 0:
+            own_copy(1).wait_recv()
+        for i in range(col * HALF, (col + 1) * HALF):
+            for d in range(2):
+                to_partner(near, 2 * d, i, NEARC + d * CHUNKS + i).wait_recv()
+
+        def after(b):
+            @pl.when(c != col)
+            def _():
+                near_image(b).start()
+
+        multiply(ids, a, near[col], out_near.at[col], after)
+
     for i in range(CHUNKS + LAG):
         if i < CHUNKS:
             @pl.when(on_edge)
@@ -300,32 +323,17 @@
             to_partner(far, 1, j, EXC + j).start()
             if j < MINE:
                 prepare(j)
+            if j == HALF:
+                near_forward(0)
             if j == CHUNKS - 2:
                 far_forward(0)
 
+    near_multiply(0)
     far_multiply(0)
     far_forward(1)
     far_multiply(1)
-
-    def near_image(b):
-        return send(out_near.at[1 - c, b], image.at[g * MINE + b], IMG + b, partner)
-
-    own_copy(1).wait_recv()
-    for col in range(2):
-        for i in range(col * HALF, (col + 1) * HALF):
-            for d in range(2):
-                near_halo(d, i).wait_recv()
-                to_partner(near, 2 * d, i, NEARC + d * CHUNKS + i).start()
-        for i in range(col * HALF, (col + 1) * HALF):
-            for d in range(2):
-                to_partner(near, 2 * d, i, NEARC + d * CHUNKS + i).wait_recv()
-
-        def after(b):
-            @pl.when(c != col)
-            def _():
-                near_image(b).start()
-
-        multiply(ids, a, near[col], out_near.at[col], after)
+    near_forward(1)
+    near_multiply(1)
 
     for k in range(3):
         loads[k].wait()

time: 67.9 us -> 65.3 us (0.962)
  Pallas kernels: 64.2 us -> 61.6 us
    pallas_call x1, Pallas kernels: 64.2 us -> 61.6 us  [shards(): pl.pallas_call(kernel, out_shape=(jax.ShapeDtypeStruct((BPS, BS, COLS), f...]
where the time goes in v4:
time: 65.3 us; the launch traced here: 65.2 us
  Pallas kernels  61.6 us (94%)
  local copies, waits for them, and re-layouts  2.93 us (4%)
    pallas_call x1, Pallas kernels, shards(): pl.pallas_call(kernel, out_shape=(jax.ShapeDtypeStruct((BPS, BS, COLS), f...  61.6 us
    unnamed x4, local copies, waits for them, and re-layouts  2.93 us

profile of v4, /device:TPU:1, one launch (start us, length us, event | category | flops | bytes accessed | tf_op | source)
XLA Modules:
  0.0 65.2 jit_solution(18071861871556400546)
XLA Ops:
  0.6 61.6 %chebyshev_step.1 = (f32[12,192,128]{2,1,0:T(8,128)}, f32[2,128]{1,0:T(2,128)}) custom-call(s32[12,27]{1,0:T(8,128)} %table.1, bf16[3,27,36864]{2,1,0:T(8,128)(2,1)} %tiles.1, bf16[12,192,128]{2,1,0:T(8,128)(2,1)} %t_cur.1, f32[12,192,128]{2,1,0:T(8,128)} %t_prev.1, f32[12,192,128]{2,1,0:T(8,128)} %probes.1), custom_call_target="tpu_custom_call" | custom-call | tf_op jit(solution)/shard_map/chebyshev_step/pallas_call | solution.py:430
  62.2 0.0 copy-start
  62.2 2.4 %copy.9 = f32[12,192,128]{2,1,0:T(8,128)} copy(f32[12,192,128]{2,1,0:T(8,128)} %get-tuple-element.4) | data formatting | bytes 2359296
  64.6 0.0 copy-done
  64.6 0.6 copy.10
Async XLA Ops:
  62.2 2.4 %copy-start = (f32[2,128]{1,0:T(2,128)S(1)}, f32[2,128]{1,0:T(2,128)}, u32[]{:S(2)}) copy-start(f32[2,128]{1,0:T(2,128)} %get-tuple-element.5) | copy-start | bytes 3076

commit v5 on v4

--- a/solution.py
+++ b/solution.py
@@ -108,7 +108,7 @@
 
 def kernel(
     table, tiles, t_cur, t_prev, probes, t_next, moments,
-    x, stage, a, near0, near1, far0, far1, own, out_far, out_near, image, passing, prev, probe, neighbours, ids, sums1, sums2,
+    x, stage, a, near0, near1, far0, far1, own, result, out_far, out_near, image, passing, prev, probe, neighbours, ids, sums1, sums2,
     local, ssem, rsem,
 ):
     near, far = (near0, near1), (far0, far1)
@@ -291,6 +291,8 @@
 
         multiply(ids, a, near[col], out_near.at[col], after)
 
+    prepare(0)
+
     for i in range(CHUNKS + LAG):
         if i < CHUNKS:
             @pl.when(on_edge)
@@ -321,11 +323,10 @@
                             for k in range(EARLY, CHUNKS):
                                 near_halo(d, k).start()
             to_partner(far, 1, j, EXC + j).start()
-            if j < MINE:
-                prepare(j)
-            if j == HALF:
+            if j < MINE - 1:
+                prepare(j + 1)
+            if j == CHUNKS - 1:
                 near_forward(0)
-            if j == CHUNKS - 2:
                 far_forward(0)
 
     near_multiply(0)
@@ -342,7 +343,7 @@
         def body(b, sums):
             blk = first + b
             value = 2.0 * source[at + b] - prev[blk]
-            t_next[blk] = value
+            result[blk] = value
             fold = lambda v: jnp.sum(v.reshape(BS // 8, 8, COLS), axis=0)
             return (
                 sums[0] + fold(probe[blk] * value),
@@ -361,6 +362,12 @@
         near_image(b).wait_recv()
     sums = finish_all(first, image, first, sums)
 
+    def store(k):
+        rows = pl.ds((h if k == 0 else 1 - h) * 2 * MINE, 2 * MINE)
+        return pltpu.make_async_copy(result.at[rows], t_next.at[rows], local.at[5 + MINE + k])
+
+    store(0).start()
+
     def arrived(b, sums):
         for r in range(2):
             send(out_far.at[0, b], image.at[b], IMGF + r * MINE + b, across).wait_recv()
@@ -369,6 +376,7 @@
         return sums
 
     sums = lax.fori_loop(0, MINE, arrived, sums)
+    store(1).start()
 
     top = lax.broadcasted_iota(jnp.int32, (8, COLS), 0)
     pack = lambda p, q: jnp.where(
@@ -393,6 +401,7 @@
     moments[...] = whole[0:2] * factor
 
     for p in range(2):
+        store(p).wait()
         own_copy(p).wait_send()
     for b in range(MINE):
         near_image(b).wait_send()
@@ -423,24 +432,30 @@
         copy.wait_send()
 
 
+def hand_over(value, sums, t_next, moments):
+    t_next[...] = value[...]
+    moments[...] = sums[...]
+
+
 def shards(tiles, neighbours, t_cur, t_prev, probes):
     f32, bf16 = jnp.float32, jnp.bfloat16
     anywhere = pl.BlockSpec(memory_space=pl.ANY)
     vmem = pl.BlockSpec(memory_space=pltpu.VMEM)
-    return pl.pallas_call(
+    t_next, moments = pl.pallas_call(
         kernel,
         out_shape=(
             jax.ShapeDtypeStruct((BPS, BS, COLS), f32),
             jax.ShapeDtypeStruct((2, COLS), f32),
         ),
         in_specs=[anywhere] * 5,
-        out_specs=(vmem, vmem),
+        out_specs=(anywhere, vmem),
         scratch_shapes=[
             pltpu.VMEM((MINE, NB, BS * BS), bf16),
             pltpu.VMEM((NB * PITCH, LANES), f32),
             pltpu.VMEM((MINE, BS, KPAD), bf16),
             *[pltpu.VMEM((3 * BPS, BS, COLS), bf16)] * 4,
             pltpu.VMEM((BPS, BS, COLS), bf16),
+            pltpu.VMEM((BPS, BS, COLS), f32),
             pltpu.VMEM((2, MINE, BS, COLS), f32),
             pltpu.VMEM((2, MINE, BS, COLS), f32),
             pltpu.VMEM((BPS, BS, COLS), f32),
@@ -451,7 +466,7 @@
             pltpu.SMEM((MINE * NB,), jnp.int32),
             pltpu.VMEM((8, 8, COLS), f32),
             pltpu.VMEM((8, 8, COLS), f32),
-            pltpu.SemaphoreType.DMA((5 + MINE,)),
+            pltpu.SemaphoreType.DMA((7 + MINE,)),
             pltpu.SemaphoreType.DMA((NSEM,)),
             pltpu.SemaphoreType.DMA((NSEM,)),
         ],
@@ -460,6 +475,19 @@
         ),
         name="chebyshev_step",
     )(neighbours, tiles, t_cur, t_prev, probes)
+    block = pl.BlockSpec((MINE, BS, COLS), lambda i: (i, 0, 0))
+    small = pl.BlockSpec((2, COLS), lambda i: (0, 0))
+    return pl.pallas_call(
+        hand_over,
+        grid=(BPS // MINE,),
+        out_shape=(
+            jax.ShapeDtypeStruct((BPS, BS, COLS), f32),
+            jax.ShapeDtypeStruct((2, COLS), f32),
+        ),
+        in_specs=[block, small],
+        out_specs=(block, small),
+        name="hand_over",
+    )(t_next, moments)
 
 
 def solution(mesh):

time: 65.3 us -> 66 us (1.011)
  Pallas kernels: 61.6 us -> 65.3 us
  local copies, waits for them, and re-layouts: 2.93 us -> 0 us
    pallas_call x0 -> x1, Pallas kernels: none -> 3.42 us  [shards(): pl.pallas_call(hand_over, grid=(BPS // MINE,), out_shape=(jax.ShapeDtypeS...]
    unnamed x4 -> x0, local copies, waits for them, and re-layouts: 2.93 us -> none
where the time goes in v5:
time: 66 us; the launch traced here: 65.9 us
  Pallas kernels  65.3 us (99%)
    pallas_call x1, Pallas kernels, shards(): pl.pallas_call(kernel, out_shape=(jax.ShapeDtypeStruct((BPS, BS, COLS), f...  61.8 us
    pallas_call x1, Pallas kernels, shards(): pl.pallas_call(hand_over, grid=(BPS // MINE,), out_shape=(jax.ShapeDtypeS...  3.42 us

profile of v5, /device:TPU:1, one launch (start us, length us, event | category | flops | bytes accessed | tf_op | source)
XLA Modules:
  0.0 65.9 jit_solution(1437578616126486847)
XLA Ops:
  0.6 61.8 %chebyshev_step.1 = (f32[12,192,128]{2,1,0:T(8,128)}, f32[2,128]{1,0:T(2,128)}) custom-call(s32[12,27]{1,0:T(8,128)} %table.1, bf16[3,27,36864]{2,1,0:T(8,128)(2,1)} %tiles.1, bf16[12,192,128]{2,1,0:T(8,128)(2,1)} %t_cur.1, f32[12,192,128]{2,1,0:T(8,128)} %t_prev.1, f32[12,192,128]{2,1,0:T(8,128)} %probes.1), custom_call_target="tpu_custom_call" | custom-call | tf_op jit(solution)/shard_map/chebyshev_step/pallas_call | solution.py:444
  62.5 3.4 %hand_over.1 = (f32[12,192,128]{2,1,0:T(8,128)}, f32[2,128]{1,0:T(2,128)}) custom-call(f32[12,192,128]{2,1,0:T(8,128)} %get-tuple-element.4.value, f32[2,128]{1,0:T(2,128)} %get-tuple-element.5.sums), custom_call_target="tpu_custom_call" | custom-call | tf_op jit(solution)/shard_map/hand_over/pallas_call | solution.py:480

commit v6 on v4

--- a/solution.py
+++ b/solution.py
@@ -108,7 +108,7 @@
 
 def kernel(
     table, tiles, t_cur, t_prev, probes, t_next, moments,
-    x, stage, a, near0, near1, far0, far1, own, out_far, out_near, image, passing, prev, probe, neighbours, ids, sums1, sums2,
+    x, stage, a, near0, near1, far0, far1, own, result, out_far, out_near, image, passing, prev, probe, neighbours, ids, sums1, sums2,
     local, ssem, rsem,
 ):
     near, far = (near0, near1), (far0, far1)
@@ -342,7 +342,7 @@
         def body(b, sums):
             blk = first + b
             value = 2.0 * source[at + b] - prev[blk]
-            t_next[blk] = value
+            result[blk] = value
             fold = lambda v: jnp.sum(v.reshape(BS // 8, 8, COLS), axis=0)
             return (
                 sums[0] + fold(probe[blk] * value),
@@ -361,6 +361,12 @@
         near_image(b).wait_recv()
     sums = finish_all(first, image, first, sums)
 
+    def store(k):
+        rows = pl.ds((h if k == 0 else 1 - h) * 2 * MINE, 2 * MINE)
+        return pltpu.make_async_copy(result.at[rows], t_next.at[rows], local.at[5 + MINE + k])
+
+    store(0).start()
+
     def arrived(b, sums):
         for r in range(2):
             send(out_far.at[0, b], image.at[b], IMGF + r * MINE + b, across).wait_recv()
@@ -369,6 +375,7 @@
         return sums
 
     sums = lax.fori_loop(0, MINE, arrived, sums)
+    store(1).start()
 
     top = lax.broadcasted_iota(jnp.int32, (8, COLS), 0)
     pack = lambda p, q: jnp.where(
@@ -393,6 +400,7 @@
     moments[...] = whole[0:2] * factor
 
     for p in range(2):
+        store(p).wait()
         own_copy(p).wait_send()
     for b in range(MINE):
         near_image(b).wait_send()
@@ -434,13 +442,14 @@
             jax.ShapeDtypeStruct((2, COLS), f32),
         ),
         in_specs=[anywhere] * 5,
-        out_specs=(vmem, vmem),
+        out_specs=(anywhere, vmem),
         scratch_shapes=[
             pltpu.VMEM((MINE, NB, BS * BS), bf16),
             pltpu.VMEM((NB * PITCH, LANES), f32),
             pltpu.VMEM((MINE, BS, KPAD), bf16),
             *[pltpu.VMEM((3 * BPS, BS, COLS), bf16)] * 4,
             pltpu.VMEM((BPS, BS, COLS), bf16),
+            pltpu.VMEM((BPS, BS, COLS), f32),
             pltpu.VMEM((2, MINE, BS, COLS), f32),
             pltpu.VMEM((2, MINE, BS, COLS), f32),
             pltpu.VMEM((BPS, BS, COLS), f32),
@@ -451,7 +460,7 @@
             pltpu.SMEM((MINE * NB,), jnp.int32),
             pltpu.VMEM((8, 8, COLS), f32),
             pltpu.VMEM((8, 8, COLS), f32),
-            pltpu.SemaphoreType.DMA((5 + MINE,)),
+            pltpu.SemaphoreType.DMA((7 + MINE,)),
             pltpu.SemaphoreType.DMA((NSEM,)),
             pltpu.SemaphoreType.DMA((NSEM,)),
         ],

time: 65.3 us -> 64.8 us (level)
  no operation moved by 1% of the time
where the time goes in v6:
time: 64.8 us; the launch traced here: 64.7 us
  Pallas kernels  61.1 us (94%)
  local copies, waits for them, and re-layouts  2.93 us (5%)
  between operations  0.65 us (1%)
    pallas_call x1, Pallas kernels, shards(): pl.pallas_call(kernel, out_shape=(jax.ShapeDtypeStruct((BPS, BS, COLS), f...  61.1 us
    unnamed x4, local copies, waits for them, and re-layouts  2.93 us

profile of v6, /device:TPU:1, one launch (start us, length us, event | category | flops | bytes accessed | tf_op | source)
XLA Modules:
  0.0 64.7 jit_solution(4411933461093233439)
XLA Ops:
  0.6 61.1 %chebyshev_step.1 = (f32[12,192,128]{2,1,0:T(8,128)}, f32[2,128]{1,0:T(2,128)}) custom-call(s32[12,27]{1,0:T(8,128)} %table.1, bf16[3,27,36864]{2,1,0:T(8,128)(2,1)} %tiles.1, bf16[12,192,128]{2,1,0:T(8,128)(2,1)} %t_cur.1, f32[12,192,128]{2,1,0:T(8,128)} %t_prev.1, f32[12,192,128]{2,1,0:T(8,128)} %probes.1), custom_call_target="tpu_custom_call" | custom-call | tf_op jit(solution)/shard_map/chebyshev_step/pallas_call | solution.py:438
  61.8 0.0 copy-start
  61.8 2.4 %copy.9 = f32[12,192,128]{2,1,0:T(8,128)} copy(f32[12,192,128]{2,1,0:T(8,128)} %get-tuple-element.4) | data formatting | bytes 2359296
  64.2 0.0 copy-done
  64.2 0.6 copy.10
Async XLA Ops:
  61.8 2.4 %copy-start = (f32[2,128]{1,0:T(2,128)S(1)}, f32[2,128]{1,0:T(2,128)}, u32[]{:S(2)}) copy-start(f32[2,128]{1,0:T(2,128)} %get-tuple-element.5) | copy-start | bytes 3076
